TPU v7x, 32 devices: a whole 2x2x4 slice. The times are simulated.
32 devices in a mesh: grp: 4 (over y, x), slab: 8 (over z, core).
Axes of the slice: x: 2, y: 2, z: 4, core: 2. Of those that a mesh axis runs over, the one named last changes fastest.
Arguments:
- fields: float32 [64, 64, 8, 128], P('grp', 'slab'), may hold values from -6 to 6
- velocity: int32 [3, 64, 8, 128], P(None, 'slab'), may hold values from -2 to 2
- diffusivity: float32 [64, 8, 128], P('slab'), may hold values from 0.005 to 0.04
- sensor_offsets: int32 [49152], P('slab'), may hold values from 0 to 8191
- sensor_counts: int32 [8], P('slab'), may hold values from 1 to 6144, 16384 in all
- observations: float32 [49152], P('slab'), may hold values from -6 to 6
- noise_scale: float32 [49152], P('slab'), may hold values from 2 to 20
- perturbation: float32 [64, 49152], P('grp', 'slab'), may hold values from -6 to 6
Outputs:
- updated: float32 [64, 64, 8, 128], P('grp', 'slab')
Inputs may be any that keep to these rules, and one draw needn't show every extreme that they name: `sensor_counts`: the counts sum to 16384 and the largest is exactly 6144. `sensor_offsets`: slots at or past their slab's count are unused.
All inputs are finite; a program needn't handle non-finite values. No bound on the sum of `sensor_counts` on one device may be relied on, other than what follows from the above.
Results may differ from a plain program's by a relative error of at most 0.00011.
Values sent between devices are 32-bit elements; how exact they have to be, the bound alone decides.
A program may use at most 64 MiB of HBM per device.

v0:
```python
import math
import jax
import jax.numpy as jnp
from jax import lax
from jax.sharding import PartitionSpec as P

STEPS = 2
COURANT = 0.12


def extended_2(array, sides, width):
    for axis, dim in sides:
        size, length = (lax.axis_size(axis), array.shape[dim])
        up = [(i, (i + 1) % size) for i in range(size - 1)]
        down = [(j, i) for i, j in up]
        last = lax.slice_in_dim(array, length - width, length, axis=dim)
        initial = lax.slice_in_dim(array, 0, width, axis=dim)
        before = lax.ppermute(last, axis, up)
        after = lax.ppermute(initial, axis, down)
        array = jnp.concatenate([before, array, after], axis=dim)
    return array


def upwind(courant, center, lower_side, upper_side):
    return jnp.maximum(courant, 0.0) * (center - lower_side) + jnp.minimum(courant, 0.0) * (
        upper_side - center
    )


def advance(extended, courant, diffusivity):
    center = extended[:, 1:-1]
    below = extended[:, :-2]
    above = extended[:, 2:]
    south = jnp.roll(center, 1, axis=2)
    north = jnp.roll(center, -1, axis=2)
    west = jnp.roll(center, 1, axis=3)
    east = jnp.roll(center, -1, axis=3)
    transport = upwind(courant[0], center, below, above) + upwind(courant[1], center, south, north)
    transport = transport + upwind(courant[2], center, west, east)
    laplace = below + above + south + north + west + east - 6.0 * center
    return center - transport + diffusivity * laplace


def solve_weights(gram_matrix, cross_matrix, spread_root):
    order = gram_matrix.shape[0]
    index_row = jnp.arange(order, dtype=jnp.int32)
    system = jnp.eye(order, dtype=jnp.float32) + gram_matrix

    def factor_column(column, lower_factor):
        row_here = lax.dynamic_slice_in_dim(lower_factor, column, 1, 0)[0]
        needed = lax.dynamic_slice_in_dim(system, column, 1, 1)[:, 0]
        needed = needed - jnp.dot(
            lower_factor,
            row_here,
            precision=lax.Precision.HIGHEST,
            preferred_element_type=jnp.float32,
        )
        pivot = jnp.sqrt(lax.dynamic_slice_in_dim(needed, column, 1, 0)[0])
        values = jnp.where(index_row >= column, needed / pivot, 0.0)
        marker = (index_row == column).astype(jnp.float32)
        return lower_factor + values[:, None] * marker[None, :]

    lower_factor = lax.fori_loop(0, order, factor_column, jnp.zeros((order, order), jnp.float32))

    def forward_row(row, solved):
        factor_row = lax.dynamic_slice_in_dim(lower_factor, row, 1, 0)[0]
        pivot = lax.dynamic_slice_in_dim(factor_row, row, 1, 0)[0]
        given = lax.dynamic_slice_in_dim(cross_matrix, row, 1, 0)[0]
        value = (
            given
            - jnp.dot(
                factor_row,
                solved,
                precision=lax.Precision.HIGHEST,
                preferred_element_type=jnp.float32,
            )
        ) / pivot
        return lax.dynamic_update_slice_in_dim(solved, value[None, :], row, 0)

    middle = lax.fori_loop(0, order, forward_row, jnp.zeros_like(cross_matrix))

    def backward_row(turn, solved):
        row = order - 1 - turn
        factor_col = lax.dynamic_slice_in_dim(lower_factor, row, 1, 1)[:, 0]
        pivot = lax.dynamic_slice_in_dim(factor_col, row, 1, 0)[0]
        given = lax.dynamic_slice_in_dim(middle, row, 1, 0)[0]
        value = (
            given
            - jnp.dot(
                factor_col,
                solved,
                precision=lax.Precision.HIGHEST,
                preferred_element_type=jnp.float32,
            )
        ) / pivot
        return lax.dynamic_update_slice_in_dim(solved, value[None, :], row, 0)

    result = lax.fori_loop(0, order, backward_row, jnp.zeros_like(cross_matrix))
    return result / spread_root


def ensemble_parts(centered, misfit_rows):
    gram_part = jnp.dot(
        centered, centered.T, precision=lax.Precision.HIGHEST, preferred_element_type=jnp.float32
    )
    cross_part = jnp.dot(
        centered, misfit_rows.T, precision=lax.Precision.HIGHEST, preferred_element_type=jnp.float32
    )
    return (gram_part, cross_part)


def sample_cells(current, sensor_offsets):
    members_here = current.shape[0]
    row_count = current.shape[1] * current.shape[2]
    width = current.shape[3]
    planes = current.reshape(members_here, row_count, width)
    slot_total = sensor_offsets.shape[0]
    block_size = math.gcd(slot_total, 512)
    block_count = slot_total // block_size
    row_ids = jnp.arange(row_count, dtype=jnp.int32)
    col_ids = jnp.arange(width, dtype=jnp.int32)

    def pick_block(offsets):
        row_pick = offsets // width
        col_pick = offsets % width
        col_table = (col_ids[:, None] == col_pick[None, :]).astype(jnp.float32)
        chosen = jnp.einsum(
            "qng,gl->qnl",
            planes,
            col_table,
            precision=lax.Precision.HIGHEST,
            preferred_element_type=jnp.float32,
        )
        row_table = (row_ids[:, None] == row_pick[None, :]).astype(jnp.float32)
        return jnp.sum(chosen * row_table[None, :, :], axis=1)

    blocks = lax.map(pick_block, sensor_offsets.reshape(block_count, block_size))
    return jnp.transpose(blocks, (1, 0, 2)).reshape(members_here, slot_total)


def local(
    fields,
    velocity,
    diffusivity,
    sensor_offsets,
    sensor_counts,
    observations,
    noise_scale,
    perturbation,
):
    members_here = fields.shape[0]
    group_count = lax.axis_size("grp")
    members_all = members_here * group_count
    spread_root = math.sqrt(members_all - 1)
    courant = velocity.astype(jnp.float32) * COURANT
    current = fields
    for counter in range(STEPS):
        extended = extended_2(current, (("slab", 1),), 1)
        current = advance(extended, courant, diffusivity)
    cell_total = current.shape[1] * current.shape[2] * current.shape[3]
    flattened = current.reshape(members_here, cell_total)
    slot_total = sensor_offsets.shape[0]
    live_mask = (jnp.arange(slot_total, dtype=jnp.int32) < sensor_counts[0]).astype(jnp.float32)
    predicted = sample_cells(current, sensor_offsets)
    scaled = live_mask * predicted / noise_scale
    misfit = live_mask * ((observations - predicted) / noise_scale + perturbation)
    scaled_sum = lax.psum(jnp.sum(scaled, axis=0), "grp")
    leading = (scaled - scaled_sum / members_all) / spread_root
    gathered_lead, gathered_misfit = (
        lax.all_gather(leading, "grp", axis=0, tiled=True),
        lax.all_gather(misfit, "grp", axis=0, tiled=True),
    )
    gram_part, cross_part = ensemble_parts(gathered_lead, gathered_misfit)
    gram_matrix, cross_matrix = lax.psum((gram_part, cross_part), "slab")
    weights = solve_weights(gram_matrix, cross_matrix, spread_root)
    group_index = lax.axis_index("grp")
    own_weights = lax.dynamic_slice_in_dim(weights, group_index * members_here, members_here, 1)
    increment = jnp.dot(
        own_weights.T,
        lax.all_gather(flattened, "grp", axis=0, tiled=True),
        precision=lax.Precision.HIGHEST,
        preferred_element_type=jnp.float32,
    )
    return (flattened + increment).reshape(current.shape)


def solution(mesh):
    return jax.shard_map(
        local,
        mesh=mesh,
        in_specs=(
            P("grp", "slab", None, None),
            P(None, "slab", None, None),
            P("slab", None, None),
            P("slab"),
            P("slab"),
            P("slab"),
            P("slab"),
            P("grp", "slab"),
        ),
        out_specs=P("grp", "slab", None, None),
        check_vma=False,
    )
```

profile of v0, /device:TPU:0, one launch (start us, length us, event | category | flops | bytes accessed | tf_op | source)
XLA Modules:
  0.0 487.9 jit_solution(3557998516879532501)
XLA Ops:
  6.5 1.6 fusion.75
  8.1 3.0 collective-permute-start
  11.1 1.3 collective-permute-start.1
  12.4 1.3 fusion.72
  13.9 1.0 fusion.74
  15.7 0.9 convert_multiply_fusion
  17.3 1.3 reshape.81
  19.9 1.4 div.111
  21.9 2.0 fusion.51
  24.5 4.6 collective-permute-start.2
  29.1 1.3 collective-permute-start.3
  30.5 3.0 collective-permute-done.3
  34.4 31.0 %while.62 = (s32[]{:T(128)}, f32[12,16,512]{2,1,0:T(8,128)S(1)}, s32[12,512]{1,0:T(8,128)}, f32[16,64,128]{2,1,0:T(8,128)S(1)}, s32[]{:T(128)}) while((s32[]{:T(128)}, f32[12,16,512]{2,1,0:T(8,128)S(1)}, s32[12,512]{1,0:T(8,128)}, f32[16,64,128]{2,1,0:T(8,128)S(1)}, s32[]{:T(128)}) %tuple.168), condition=%wide.region_2.3_spmd.clone, body=%wide.region_0.2_spmd.clone.sunk | while | flops 806489600 | bytes 901193 | solution.py:137
  35.9 1.0 fusion.109
  38.5 1.0 fusion.109
  41.1 1.0 fusion.109
  43.7 1.0 fusion.109
  46.3 1.0 fusion.109
  48.9 1.1 fusion.109
  51.5 1.0 fusion.109
  54.0 1.0 fusion.109
  56.6 1.0 fusion.109
  59.2 1.1 fusion.109
  61.8 1.0 fusion.109
  64.4 1.0 fusion.109
  65.7 16.3 %psum.21 = f32[6144]{0:T(1024)S(1)} all-reduce(f32[6144]{0:T(1024)S(1)} %reduce_sum.24), channel_id=1, replica_groups=mesh['grp'=4,'slab'=8] {'grp'}, use_global_device_ids=true, to_apply=%region_4.5 | all-reduce | flops 6144 | bytes 49152 | tf_op jit(solution)/shard_map/psum | solution.py:167
  82.0 1.0 add_multiply_fusion
  83.8 1.1 copy.20
  85.0 29.7 %all-gather.4.cloned.1.call-done = f32[64,6144]{1,0:T(8,128)} async-done(((f32[16,6144]{1,0:T(8,128)}), f32[64,6144]{1,0:T(8,128)}) %all-gather.4.cloned.1.call-update) | async-done | bytes 1572880 | tf_op jit(solution)/shard_map/all_gather | solution.py:170
  114.6 3.4 fusion.77
  118.0 29.3 %all-gather.6.cloned.1.call-done = f32[64,6144]{1,0:T(8,128)} async-done(((f32[16,6144]{1,0:T(8,128)}), f32[64,6144]{1,0:T(8,128)}) %all-gather.6.cloned.1.call-update) | async-done | bytes 1572880 | tf_op jit(solution)/shard_map/all_gather | solution.py:171
  147.3 2.8 fusion.76
  150.1 28.9 %all-reduce = (f32[64,64]{1,0:T(8,128)S(1)}, f32[64,64]{1,0:T(8,128)S(1)}) all-reduce(f32[64,64]{1,0:T(8,128)S(1)} %fusion.76, f32[64,64]{1,0:T(8,128)S(1)} %fusion.77), channel_id=1, replica_groups=mesh['grp'=4,'slab'=8] {'slab'}, use_global_device_ids=true, to_apply=%region_8.9 | all-reduce | flops 8192 | bytes 65536 | tf_op jit(solution)/shard_map/psum | solution.py:174
  179.1 105.9 %while.63 = (s32[]{:T(128)}, f32[64,64]{1,0:T(8,128)S(1)}, f32[64,64]{0,1:T(8,128)S(1)}, s32[]{:T(128)}, s32[]{:T(128)}) while((s32[]{:T(128)}, f32[64,64]{1,0:T(8,128)S(1)}, f32[64,64]{0,1:T(8,128)S(1)}, s32[]{:T(128)}, s32[]{:T(128)}) %tuple.153), condition=%wide.region_7.8_spmd.clone.clone, body=%wide.region_6.7_spmd.clone.clone.sunk | while | flops 65923 | bytes 101992 | solution.py:63
  285.1 96.0 %while.60 = (s32[]{:T(128)}, f32[64,64]{1,0:T(8,128)S(1)}, f32[64,64]{1,0:T(8,128)S(1)}, f32[64,64]{1,0:T(8,128)S(1)}, s32[]{:T(128)}, /*index=5*/s32[]{:T(128)}, s32[]{:T(128)}) while((s32[]{:T(128)}, f32[64,64]{1,0:T(8,128)S(1)}, f32[64,64]{1,0:T(8,128)S(1)}, f32[64,64]{1,0:T(8,128)S(1)}, s32[]{:T(128)}, /*index=5*/s32[]{:T(128)}, ...), condition=%wide.region_10.11_spmd, body=%wide.region_9.10_spmd.sunk | while | flops 49283 | bytes 36205 | solution.py:80
  285.8 0.8 fusion.102
  287.3 0.8 fusion.102
  288.8 0.8 fusion.102
  290.3 0.8 fusion.102
  291.8 0.8 fusion.102
  293.3 0.8 fusion.102
  294.8 0.8 fusion.102
  297.8 0.8 fusion.102
  299.3 0.8 fusion.102
  302.3 0.8 fusion.102
  303.8 0.8 fusion.102
  306.8 0.8 fusion.102
  308.3 0.8 fusion.102
  309.8 0.8 fusion.102
  311.3 0.8 fusion.102
  312.8 0.8 fusion.102
  314.3 0.8 fusion.102
  315.8 0.8 fusion.102
  317.3 0.8 fusion.102
  318.8 0.8 fusion.102
  320.3 0.8 fusion.102
  321.8 0.8 fusion.102
  323.3 0.8 fusion.102
  326.3 0.8 fusion.102
  327.8 0.8 fusion.102
  330.8 0.8 fusion.102
  381.1 96.4 %while.61 = (s32[]{:T(128)}, f32[64,64]{1,0:T(8,128)S(1)}, f32[64,64]{1,0:T(8,128)S(1)}, f32[64,64]{0,1:T(8,128)S(1)}, s32[]{:T(128)}, /*index=5*/s32[]{:T(128)}, s32[]{:T(128)}, s32[]{:T(128)}) while((s32[]{:T(128)}, f32[64,64]{1,0:T(8,128)S(1)}, f32[64,64]{1,0:T(8,128)S(1)}, f32[64,64]{0,1:T(8,128)S(1)}, s32[]{:T(128)}, ...), condition=%wide.region_12.13_spmd, body=%wide.region_11.12_spmd.sunk | while | flops 49287 | bytes 35751 | solution.py:98
  477.6 2.9 fusion.26
  480.5 0.9 copy.16
  (852 shorter events, 250.8 us)
Async XLA Ops:
  6.5 7.2 %copy-start = (f32[16,8,8,128]{3,2,1,0:T(8,128)S(1)}, f32[16,8,8,128]{3,2,1,0:T(8,128)}, u32[]{:S(2)}) copy-start(f32[16,8,8,128]{3,2,1,0:T(8,128)} %param.16) | copy-start | bytes 1572868
  6.5 108.1 %all-gather.4.cloned.1.call-start = ((), (), s32[]{:S(2)}) async-start(), calls=%async_computation | async-start | bytes 1966080 | tf_op jit(solution)/shard_map/all_gather | solution.py:170
  8.1 13.8 %collective-permute-start = (f32[16,1,8,128]{3,2,1,0:T(8,128)}, f32[16,1,8,128]{3,2,1,0:T(8,128)}, u32[]{:S(2)}, u32[]{:S(2)}) collective-permute-start(f32[16,1,8,128]{3,2,1,0:T(8,128)} %get-tuple-element.525), channel_id=1, source_target_pairs={{0,1},{1,2},{2,3},{3,4},{4,5},{5,6},{6,7},{8,9},{9,10},{10,11},{11... | collective-permute-start | bytes 196616 | tf_op jit(solution)/shard_map/ppermute | solution.py:18
  11.1 10.7 %collective-permute-start.1 = (f32[16,1,8,128]{3,2,1,0:T(8,128)}, f32[16,1,8,128]{3,2,1,0:T(8,128)}, u32[]{:S(2)}, u32[]{:S(2)}) collective-permute-start(f32[16,1,8,128]{3,2,1,0:T(8,128)} %get-tuple-element.526), channel_id=1, source_target_pairs={{1,0},{2,1},{3,2},{4,3},{5,4},{6,5},{7,6},{9,8},{10,9},{11,10},{12... | collective-permute-start | bytes 196616 | tf_op jit(solution)/shard_map/ppermute | solution.py:19
  24.2 9.3 %copy-start.3 = (f32[8,8,128]{2,1,0:T(8,128)S(1)}, f32[8,8,128]{2,1,0:T(8,128)}, u32[]{:S(2)}) copy-start(f32[8,8,128]{2,1,0:T(8,128)} %get-tuple-element.529) | copy-start | bytes 98308
  24.2 9.3 %copy-start.4 = (f32[8,8,128]{2,1,0:T(8,128)S(1)}, f32[8,8,128]{2,1,0:T(8,128)}, u32[]{:S(2)}) copy-start(f32[8,8,128]{2,1,0:T(8,128)} %get-tuple-element.530) | copy-start | bytes 98308
  24.2 9.3 %copy-start.5 = (f32[8,8,128]{2,1,0:T(8,128)S(1)}, f32[8,8,128]{2,1,0:T(8,128)}, u32[]{:S(2)}) copy-start(f32[8,8,128]{2,1,0:T(8,128)} %get-tuple-element.531) | copy-start | bytes 98308
  24.2 9.3 %copy-start.6 = (f32[8,8,128]{2,1,0:T(8,128)S(1)}, f32[8,8,128]{2,1,0:T(8,128)}, u32[]{:S(2)}) copy-start(f32[8,8,128]{2,1,0:T(8,128)} %get-tuple-element.532) | copy-start | bytes 98308
  24.3 9.3 %copy-start.7 = (f32[8,8,128]{2,1,0:T(8,128)S(1)}, f32[8,8,128]{2,1,0:T(8,128)}, u32[]{:S(2)}) copy-start(f32[8,8,128]{2,1,0:T(8,128)} %get-tuple-element.533) | copy-start | bytes 98308
  24.3 9.3 %copy-start.8 = (f32[8,8,128]{2,1,0:T(8,128)S(1)}, f32[8,8,128]{2,1,0:T(8,128)}, u32[]{:S(2)}) copy-start(f32[8,8,128]{2,1,0:T(8,128)} %get-tuple-element.534) | copy-start | bytes 98308
  24.3 9.3 %copy-start.9 = (f32[8,8,128]{2,1,0:T(8,128)S(1)}, f32[8,8,128]{2,1,0:T(8,128)}, u32[]{:S(2)}) copy-start(f32[8,8,128]{2,1,0:T(8,128)} %param.18) | copy-start | bytes 98308
  24.5 6.0 %collective-permute-start.2 = (f32[16,1,8,128]{3,2,1,0:T(8,128)S(1)}, f32[16,1,8,128]{3,2,1,0:T(8,128)S(1)}, u32[]{:S(2)}, u32[]{:S(2)}) collective-permute-start(f32[16,1,8,128]{3,2,1,0:T(8,128)S(1)} %get-tuple-element.515), channel_id=1, source_target_pairs={{0,1},{1,2},{2,3},{3,4},{4,5},{5,6},{6,7},{8,9},{9,10},{10,11},{11... | collective-permute-start | bytes 196616 | tf_op jit(solution)/shard_map/ppermute | solution.py:18
  29.1 4.4 collective-permute-start.3
  34.4 31.1 %copy-start.10 = (f32[12,512]{1,0:T(8,128)S(1)}, f32[12,512]{1,0:T(8,128)}, u32[]{:S(2)}) copy-start(f32[12,512]{1,0:T(8,128)} %fusion.61) | copy-start | bytes 73732
  34.4 31.1 %copy-start.11 = (f32[12,512]{1,0:T(8,128)S(1)}, f32[12,512]{1,0:T(8,128)}, u32[]{:S(2)}) copy-start(f32[12,512]{1,0:T(8,128)} %div.111) | copy-start | bytes 73732
  34.4 47.5 %copy-start.12 = (f32[6144]{0:T(1024)S(1)}, f32[6144]{0:T(1024)}, u32[]{:S(2)}) copy-start(f32[6144]{0:T(1024)} %param.22) | copy-start | bytes 73732
  34.4 47.5 %copy-start.13 = (f32[6144]{0:T(1024)S(1)}, f32[6144]{0:T(1024)}, u32[]{:S(2)}) copy-start(f32[6144]{0:T(1024)} %fusion.62) | copy-start | bytes 73732
  34.4 47.5 %copy-start.14 = (f32[6144]{0:T(1024)S(1)}, f32[6144]{0:T(1024)}, u32[]{:S(2)}) copy-start(f32[6144]{0:T(1024)} %param.21) | copy-start | bytes 73732
  65.5 16.5 %copy-start.2 = (f32[16,6144]{1,0:T(8,128)S(1)}, f32[16,6144]{1,0:T(8,128)}, u32[]{:S(2)}) copy-start(f32[16,6144]{1,0:T(8,128)} %param.23) | copy-start | bytes 1179652
  83.0 64.3 %all-gather.6.cloned.1.call-start = ((), (), s32[]{:S(2)}) async-start(), calls=%async_computation.1 | async-start | bytes 1966080 | tf_op jit(solution)/shard_map/all_gather | solution.py:171
  83.8 393.8 %all-gather.8.cloned.1.call-start = ((), (), s32[]{:S(2)}) async-start(), calls=%async_computation.2 | async-start | bytes 2621440 | tf_op jit(solution)/shard_map/all_gather | solution.py:180
  114.6 32.7 %copy-start.1 = (f32[64,6144]{1,0:T(8,128)S(1)}, f32[64,6144]{1,0:T(8,128)}, u32[]{:S(2)}) copy-start(f32[64,6144]{1,0:T(8,128)} %all-gather.4.cloned.1.call-done) | copy-start | bytes 4718596
Sparse Core Ops, SparseCore 0:
  83.1 31.4 all-gather.3
  116.5 30.8 all-gather.5
  149.2 35.2 all-gather.7
where the time goes:
time: 492 us; the launch traced here: 488 us
  local copies, waits for them, and re-layouts  140 us (28%)
  matrix products  134 us (27%)
  waiting for transfers between devices  62.7 us (13%)
  loops' own time  50.6 us (10%)
  blocking collectives  45.2 us (9%)
  other arithmetic  30.7 us (6%)
  between operations  14.2 us (3%)
  starting transfers between devices  10.3 us (2%)
    dot_general x64, matrix products, forward_row(): jnp.dot(factor_row, solved, precision=lax.Precision.HIGHEST, preferred_el...  51.5 us
    dot_general x64, matrix products, backward_row(): jnp.dot(factor_col, solved, precision=lax.Precision.HIGHEST, preferred_el...  51.5 us
    another operation x1, loops' own time, solve_weights(): lax.fori_loop(0, order, factor_column, jnp.zeros((order, order), jnp.floa...  47.1 us
    dynamic_slice x64, local copies, waits for them, and re-layouts, factor_column(): pivot = jnp.sqrt(lax.dynamic_slice_in_dim(needed, column, 1, 0)[0])  43.5 us
    dynamic_slice x64, local copies, waits for them, and re-layouts, forward_row(): pivot = lax.dynamic_slice_in_dim(factor_row, row, 1, 0)[0]  41.6 us
    dynamic_slice x64, local copies, waits for them, and re-layouts, backward_row(): pivot = lax.dynamic_slice_in_dim(factor_col, row, 1, 0)[0]  41.6 us
    all_gather x1, waiting for transfers between devices, local(): lax.all_gather(leading, 'grp', axis=0, tiled=True)  29.7 us
    all_gather x1, waiting for transfers between devices, local(): lax.all_gather(misfit, 'grp', axis=0, tiled=True)  29.3 us
  transfers between devices with their start and end apart: 7, of which 3 were waited for; matrix products, arithmetic and copies ran while one was open for 54% of the time, Pallas kernels for 0%

commit v1 on v0

--- a/solution.py
+++ b/solution.py
@@ -6,6 +6,23 @@
 
 STEPS = 2
 COURANT = 0.12
+
+
+def joined_along(blocks, dim):
+    blocks = jnp.moveaxis(blocks, 0, dim)
+    lengths = blocks.shape
+    return blocks.reshape(*lengths[:dim], lengths[dim] * lengths[dim + 1], *lengths[dim + 2 :])
+
+
+def collect(x, axis, dim):
+    count = lax.axis_size(axis)
+    forward = [(i, (i + 1) % count) for i in range(count)]
+    parts = [x]
+    while len(parts) < count:
+        parts.append(lax.ppermute(parts[-1], axis, forward))
+    index = lax.axis_index(axis)
+    parts = jnp.stack(parts)[(index - jnp.arange(count)) % count]
+    return joined_along(parts, dim)
 
 
 def extended_2(array, sides, width):
@@ -168,7 +185,7 @@
     leading = (scaled - scaled_sum / members_all) / spread_root
     gathered_lead, gathered_misfit = (
         lax.all_gather(leading, "grp", axis=0, tiled=True),
-        lax.all_gather(misfit, "grp", axis=0, tiled=True),
+        collect(misfit, "grp", 0),
     )
     gram_part, cross_part = ensemble_parts(gathered_lead, gathered_misfit)
     gram_matrix, cross_matrix = lax.psum((gram_part, cross_part), "slab")

time: 492 us -> 460 us (0.935)
  waiting for transfers between devices: 62.7 us -> 45.1 us
  matrix products: 134 us -> 128 us
  local copies, waits for them, and re-layouts: 140 us -> 134 us
    ppermute x0 -> x3, waiting for transfers between devices: none -> 42 us  [collect(): parts.append(lax.ppermute(parts[-1], axis, forward))]
    all_gather x1, waiting for transfers between devices: 29.7 us -> 0.02 us  [local(): lax.all_gather(leading, 'grp', axis=0, tiled=True)]
    all_gather x1 -> x0, waiting for transfers between devices: 29.3 us -> none  [local(): lax.all_gather(misfit, 'grp', axis=0, tiled=True)]
  transfers between devices with their start and end apart: 7 -> 9, of which waited for: 3 -> 4; matrix products, arithmetic and copies ran while one was open for 54% -> 56% of each run, Pallas kernels for 0% -> 0%
where the time goes in v1:
time: 460 us; the launch traced here: 455 us
  local copies, waits for them, and re-layouts  134 us (29%)
  matrix products  128 us (28%)
  loops' own time  48.4 us (11%)
  waiting for transfers between devices  45.1 us (10%)
  blocking collectives  42.9 us (9%)
  other arithmetic  31.8 us (7%)
  between operations  14.5 us (3%)
  starting transfers between devices  10.3 us (2%)
    dot_general x64, matrix products, forward_row(): jnp.dot(factor_row, solved, precision=lax.Precision.HIGHEST, preferred_el...  49.3 us
    dot_general x64, matrix products, backward_row(): jnp.dot(factor_col, solved, precision=lax.Precision.HIGHEST, preferred_el...  49.3 us
    another operation x1, loops' own time, solve_weights(): lax.fori_loop(0, order, factor_column, jnp.zeros((order, order), jnp.floa...  44.9 us
    ppermute x3, waiting for transfers between devices, collect(): parts.append(lax.ppermute(parts[-1], axis, forward))  42 us
    dynamic_slice x64, local copies, waits for them, and re-layouts, factor_column(): pivot = jnp.sqrt(lax.dynamic_slice_in_dim(needed, column, 1, 0)[0])  41 us
    dynamic_slice x64, local copies, waits for them, and re-layouts, forward_row(): pivot = lax.dynamic_slice_in_dim(factor_row, row, 1, 0)[0]  39.1 us
    dynamic_slice x64, local copies, waits for them, and re-layouts, backward_row(): pivot = lax.dynamic_slice_in_dim(factor_col, row, 1, 0)[0]  39.1 us
    psum x1, blocking collectives, local(): gram_matrix, cross_matrix = lax.psum((gram_part, cross_part), 'slab')  26.5 us
  transfers between devices with their start and end apart: 9, of which 4 were waited for; matrix products, arithmetic and copies ran while one was open for 56% of the time, Pallas kernels for 0%

profile of v1, /device:TPU:0, one launch (start us, length us, event | category | flops | bytes accessed | tf_op | source)
XLA Modules:
  0.0 454.7 jit_solution(2769471679710333137)
XLA Ops:
  6.5 1.6 fusion.77
  8.1 3.0 collective-permute-start
  11.1 1.3 collective-permute-start.1
  12.4 1.3 fusion.74
  13.9 1.0 fusion.76
  15.7 0.9 convert_multiply_fusion
  17.3 1.3 reshape.133
  19.9 1.3 div.111
  21.8 2.0 fusion.51
  24.5 4.6 %collective-permute-start.2 = (f32[16,1,8,128]{3,2,1,0:T(8,128)S(1)}, f32[16,1,8,128]{3,2,1,0:T(8,128)S(1)}, u32[]{:S(2)}, u32[]{:S(2)}) collective-permute-start(f32[16,1,8,128]{3,2,1,0:T(8,128)S(1)} %get-tuple-element.515), channel_id=1, source_target_pairs={{0,1},{1,2},{2,3},{3,4},{4,5},{5,6},{6,7},{8,9},{9,10},{10,11},{11... | collective-permute-start | bytes 196616 | tf_op jit(solution)/shard_map/ppermute | solution.py:35
  29.1 1.3 collective-permute-start.3
  30.5 3.0 collective-permute-done.3
  33.5 0.8 fusion.35
  34.4 31.0 %while.62 = (s32[]{:T(128)}, f32[12,16,512]{2,1,0:T(8,128)S(1)}, s32[12,512]{1,0:T(8,128)}, f32[16,64,128]{2,1,0:T(8,128)S(1)}, s32[]{:T(128)}) while((s32[]{:T(128)}, f32[12,16,512]{2,1,0:T(8,128)S(1)}, s32[12,512]{1,0:T(8,128)}, f32[16,64,128]{2,1,0:T(8,128)S(1)}, s32[]{:T(128)}) %tuple.166), condition=%wide.region_2.3_spmd.clone, body=%wide.region_0.2_spmd.clone.sunk | while | flops 806489600 | bytes 901193 | solution.py:154
  35.9 1.0 fusion.111
  38.5 1.0 fusion.111
  41.1 1.1 fusion.111
  43.7 1.0 fusion.111
  46.3 1.0 fusion.111
  48.9 1.1 fusion.111
  51.4 1.0 fusion.111
  54.0 1.0 fusion.111
  56.6 1.1 fusion.111
  59.2 1.0 fusion.111
  61.8 1.0 fusion.111
  64.4 1.1 fusion.111
  65.7 16.4 %psum.21 = f32[6144]{0:T(1024)S(1)} all-reduce(f32[6144]{0:T(1024)S(1)} %reduce_sum.24), channel_id=1, replica_groups=mesh['grp'=4,'slab'=8] {'grp'}, use_global_device_ids=true, to_apply=%region_4.5 | all-reduce | flops 6144 | bytes 49152 | tf_op jit(solution)/shard_map/psum | solution.py:184
  82.1 0.9 add_multiply_fusion
  83.1 11.2 %collective-permute-done.4 = f32[16,6144]{1,0:T(8,128)S(1)} collective-permute-done((f32[16,6144]{1,0:T(8,128)S(1)}, f32[16,6144]{1,0:T(8,128)S(1)}, u32[]{:S(2)}, u32[]{:S(2)}) %collective-permute-start.4) | collective-permute-done | bytes 393248 | tf_op jit(solution)/shard_map/ppermute | solution.py:22
  94.3 13.2 %collective-permute-done.5 = f32[16,6144]{1,0:T(8,128)S(1)} collective-permute-done((f32[16,6144]{1,0:T(8,128)S(1)}, f32[16,6144]{1,0:T(8,128)S(1)}, u32[]{:S(2)}, u32[]{:S(2)}) %collective-permute-start.5) | collective-permute-done | bytes 393248 | tf_op jit(solution)/shard_map/ppermute | solution.py:22
  107.6 1.1 copy.20
  108.7 17.7 %collective-permute-done.6 = f32[16,6144]{1,0:T(8,128)} collective-permute-done((f32[16,6144]{1,0:T(8,128)S(1)}, f32[16,6144]{1,0:T(8,128)}, u32[]{:S(2)}, u32[]{:S(2)}) %collective-permute-start.6) | collective-permute-done | bytes 393248 | tf_op jit(solution)/shard_map/ppermute | solution.py:22
  126.4 1.2 pad_maximum_fusion
  128.3 3.4 fusion.79
  131.7 1.4 fusion.78
  133.1 26.5 %all-reduce = (f32[64,64]{1,0:T(8,128)S(1)}, f32[64,64]{1,0:T(8,128)S(1)}) all-reduce(f32[64,64]{1,0:T(8,128)S(1)} %fusion.78, f32[64,64]{1,0:T(8,128)S(1)} %fusion.79), channel_id=1, replica_groups=mesh['grp'=4,'slab'=8] {'slab'}, use_global_device_ids=true, to_apply=%region_8.9 | all-reduce | flops 8192 | bytes 65536 | tf_op jit(solution)/shard_map/psum | solution.py:191
  159.7 101.2 %while.63 = (s32[]{:T(128)}, f32[64,64]{1,0:T(8,128)S(1)}, f32[64,64]{0,1:T(8,128)S(1)}, s32[]{:T(128)}, s32[]{:T(128)}) while((s32[]{:T(128)}, f32[64,64]{1,0:T(8,128)S(1)}, f32[64,64]{0,1:T(8,128)S(1)}, s32[]{:T(128)}, s32[]{:T(128)}) %tuple.153), condition=%wide.region_7.8_spmd.clone.clone, body=%wide.region_6.7_spmd.clone.clone.sunk | while | flops 65923 | bytes 101992 | solution.py:80
  260.9 91.3 %while.60 = (s32[]{:T(128)}, f32[64,64]{1,0:T(8,128)S(1)}, f32[64,64]{1,0:T(8,128)S(1)}, f32[64,64]{1,0:T(8,128)S(1)}, s32[]{:T(128)}, /*index=5*/s32[]{:T(128)}, s32[]{:T(128)}) while((s32[]{:T(128)}, f32[64,64]{1,0:T(8,128)S(1)}, f32[64,64]{1,0:T(8,128)S(1)}, f32[64,64]{1,0:T(8,128)S(1)}, s32[]{:T(128)}, /*index=5*/s32[]{:T(128)}, ...), condition=%wide.region_10.11_spmd, body=%wide.region_9.10_spmd.sunk | while | flops 49283 | bytes 36205 | solution.py:97
  261.6 0.8 fusion.104
  267.3 0.8 fusion.104
  268.7 0.8 fusion.104
  274.4 0.8 fusion.104
  275.8 0.8 fusion.104
  281.5 0.8 fusion.104
  288.7 0.8 fusion.104
  294.4 0.8 fusion.104
  295.8 0.8 fusion.104
  301.5 0.8 fusion.104
  302.9 0.8 fusion.104
  308.6 0.8 fusion.104
  315.8 0.8 fusion.104
  321.5 0.8 fusion.104
  322.9 0.8 fusion.104
  328.6 0.8 fusion.104
  330.0 0.8 fusion.104
  335.7 0.8 fusion.104
  342.9 0.8 fusion.104
  348.6 0.8 fusion.104
  350.0 0.8 fusion.104
  352.3 91.8 %while.61 = (s32[]{:T(128)}, f32[64,64]{1,0:T(8,128)S(1)}, f32[64,64]{1,0:T(8,128)S(1)}, f32[64,64]{0,1:T(8,128)S(1)}, s32[]{:T(128)}, /*index=5*/s32[]{:T(128)}, s32[]{:T(128)}, s32[]{:T(128)}) while((s32[]{:T(128)}, f32[64,64]{1,0:T(8,128)S(1)}, f32[64,64]{1,0:T(8,128)S(1)}, f32[64,64]{0,1:T(8,128)S(1)}, s32[]{:T(128)}, ...), condition=%wide.region_12.13_spmd, body=%wide.region_11.12_spmd.sunk | while | flops 49287 | bytes 35751 | solution.py:115
  357.2 0.8 fusion.107
  358.6 0.8 fusion.107
  444.1 2.9 fusion.26
  447.0 0.9 copy.16
  (865 shorter events, 241.3 us)
Async XLA Ops:
  6.5 7.2 %copy-start = (f32[16,8,8,128]{3,2,1,0:T(8,128)S(1)}, f32[16,8,8,128]{3,2,1,0:T(8,128)}, u32[]{:S(2)}) copy-start(f32[16,8,8,128]{3,2,1,0:T(8,128)} %param.16) | copy-start | bytes 1572868
  6.5 121.7 %all-gather.3.cloned.1.call-start = ((), (), s32[]{:S(2)}) async-start(), calls=%async_computation | async-start | bytes 1966080 | tf_op jit(solution)/shard_map/all_gather | solution.py:187
  8.1 13.7 %collective-permute-start = (f32[16,1,8,128]{3,2,1,0:T(8,128)}, f32[16,1,8,128]{3,2,1,0:T(8,128)}, u32[]{:S(2)}, u32[]{:S(2)}) collective-permute-start(f32[16,1,8,128]{3,2,1,0:T(8,128)} %get-tuple-element.525), channel_id=1, source_target_pairs={{0,1},{1,2},{2,3},{3,4},{4,5},{5,6},{6,7},{8,9},{9,10},{10,11},{11... | collective-permute-start | bytes 196616 | tf_op jit(solution)/shard_map/ppermute | solution.py:35
  11.1 10.7 %collective-permute-start.1 = (f32[16,1,8,128]{3,2,1,0:T(8,128)}, f32[16,1,8,128]{3,2,1,0:T(8,128)}, u32[]{:S(2)}, u32[]{:S(2)}) collective-permute-start(f32[16,1,8,128]{3,2,1,0:T(8,128)} %get-tuple-element.526), channel_id=1, source_target_pairs={{1,0},{2,1},{3,2},{4,3},{5,4},{6,5},{7,6},{9,8},{10,9},{11,10},{12... | collective-permute-start | bytes 196616 | tf_op jit(solution)/shard_map/ppermute | solution.py:36
  24.2 9.3 %copy-start.6 = (f32[8,8,128]{2,1,0:T(8,128)S(1)}, f32[8,8,128]{2,1,0:T(8,128)}, u32[]{:S(2)}) copy-start(f32[8,8,128]{2,1,0:T(8,128)} %get-tuple-element.529) | copy-start | bytes 98308
  24.2 9.3 %copy-start.7 = (f32[8,8,128]{2,1,0:T(8,128)S(1)}, f32[8,8,128]{2,1,0:T(8,128)}, u32[]{:S(2)}) copy-start(f32[8,8,128]{2,1,0:T(8,128)} %get-tuple-element.530) | copy-start | bytes 98308
  24.2 9.3 %copy-start.8 = (f32[8,8,128]{2,1,0:T(8,128)S(1)}, f32[8,8,128]{2,1,0:T(8,128)}, u32[]{:S(2)}) copy-start(f32[8,8,128]{2,1,0:T(8,128)} %get-tuple-element.531) | copy-start | bytes 98308
  24.2 9.3 %copy-start.9 = (f32[8,8,128]{2,1,0:T(8,128)S(1)}, f32[8,8,128]{2,1,0:T(8,128)}, u32[]{:S(2)}) copy-start(f32[8,8,128]{2,1,0:T(8,128)} %get-tuple-element.532) | copy-start | bytes 98308
  24.2 9.3 %copy-start.10 = (f32[8,8,128]{2,1,0:T(8,128)S(1)}, f32[8,8,128]{2,1,0:T(8,128)}, u32[]{:S(2)}) copy-start(f32[8,8,128]{2,1,0:T(8,128)} %get-tuple-element.533) | copy-start | bytes 98308
  24.2 9.3 %copy-start.11 = (f32[8,8,128]{2,1,0:T(8,128)S(1)}, f32[8,8,128]{2,1,0:T(8,128)}, u32[]{:S(2)}) copy-start(f32[8,8,128]{2,1,0:T(8,128)} %get-tuple-element.534) | copy-start | bytes 98308
  24.2 9.3 %copy-start.12 = (f32[8,8,128]{2,1,0:T(8,128)S(1)}, f32[8,8,128]{2,1,0:T(8,128)}, u32[]{:S(2)}) copy-start(f32[8,8,128]{2,1,0:T(8,128)} %param.18) | copy-start | bytes 98308
  24.5 6.0 %collective-permute-start.2 = (f32[16,1,8,128]{3,2,1,0:T(8,128)S(1)}, f32[16,1,8,128]{3,2,1,0:T(8,128)S(1)}, u32[]{:S(2)}, u32[]{:S(2)}) collective-permute-start(f32[16,1,8,128]{3,2,1,0:T(8,128)S(1)} %get-tuple-element.515), channel_id=1, source_target_pairs={{0,1},{1,2},{2,3},{3,4},{4,5},{5,6},{6,7},{8,9},{9,10},{10,11},{11... | collective-permute-start | bytes 196616 | tf_op jit(solution)/shard_map/ppermute | solution.py:35
  29.1 4.4 collective-permute-start.3
  34.4 31.2 %copy-start.13 = (f32[12,512]{1,0:T(8,128)S(1)}, f32[12,512]{1,0:T(8,128)}, u32[]{:S(2)}) copy-start(f32[12,512]{1,0:T(8,128)} %fusion.61) | copy-start | bytes 73732
  34.4 31.2 %copy-start.14 = (f32[12,512]{1,0:T(8,128)S(1)}, f32[12,512]{1,0:T(8,128)}, u32[]{:S(2)}) copy-start(f32[12,512]{1,0:T(8,128)} %div.111) | copy-start | bytes 73732
  34.4 47.7 %copy-start.15 = (f32[6144]{0:T(1024)S(1)}, f32[6144]{0:T(1024)}, u32[]{:S(2)}) copy-start(f32[6144]{0:T(1024)} %param.22) | copy-start | bytes 73732
  34.4 47.7 %copy-start.16 = (f32[6144]{0:T(1024)S(1)}, f32[6144]{0:T(1024)}, u32[]{:S(2)}) copy-start(f32[6144]{0:T(1024)} %fusion.62) | copy-start | bytes 73732
  34.4 47.7 %copy-start.17 = (f32[6144]{0:T(1024)S(1)}, f32[6144]{0:T(1024)}, u32[]{:S(2)}) copy-start(f32[6144]{0:T(1024)} %param.21) | copy-start | bytes 73732
  65.4 42.1 %copy-start.2 = (f32[16,64,128]{2,1,0:T(8,128)}, f32[16,64,128]{2,1,0:T(8,128)S(1)}, u32[]{:S(2)}) copy-start(f32[16,64,128]{2,1,0:T(8,128)S(1)} %get-tuple-element.711) | copy-start | bytes 1572868
  65.5 16.6 %copy-start.5 = (f32[16,6144]{1,0:T(8,128)S(1)}, f32[16,6144]{1,0:T(8,128)}, u32[]{:S(2)}) copy-start(f32[16,6144]{1,0:T(8,128)} %param.23) | copy-start | bytes 1179652
  83.0 361.0 %all-gather.5.cloned.1.call-start = ((), (), s32[]{:S(2)}) async-start(), calls=%async_computation.1 | async-start | bytes 2621440 | tf_op jit(solution)/shard_map/all_gather | solution.py:197
  83.1 11.2 %collective-permute-start.4 = (f32[16,6144]{1,0:T(8,128)S(1)}, f32[16,6144]{1,0:T(8,128)S(1)}, u32[]{:S(2)}, u32[]{:S(2)}) collective-permute-start(f32[16,6144]{1,0:T(8,128)S(1)} %get-tuple-element.527), channel_id=1, source_target_pairs={{0,8},{8,16},{16,24},{24,0},{1,9},{9,17},{17,25},{25,1},{2,10},{10... | collective-permute-start | bytes 1179656 | tf_op jit(solution)/shard_map/ppermute | solution.py:22
  94.3 13.2 %collective-permute-start.5 = (f32[16,6144]{1,0:T(8,128)S(1)}, f32[16,6144]{1,0:T(8,128)S(1)}, u32[]{:S(2)}, u32[]{:S(2)}) collective-permute-start(f32[16,6144]{1,0:T(8,128)S(1)} %collective-permute-done.4), channel_id=1, source_target_pairs={{0,8},{8,16},{16,24},{24,0},{1,9},{9,17},{17,25},{25,1},{2,10},{10... | collective-permute-start | bytes 1179656 | tf_op jit(solution)/shard_map/ppermute | solution.py:22
  107.5 18.8 %copy-start.4 = (f32[16,6144]{1,0:T(8,128)}, f32[16,6144]{1,0:T(8,128)S(1)}, u32[]{:S(2)}) copy-start(f32[16,6144]{1,0:T(8,128)S(1)} %collective-permute-done.5) | copy-start | bytes 1179652
  107.5 18.8 %collective-permute-start.6 = (f32[16,6144]{1,0:T(8,128)S(1)}, f32[16,6144]{1,0:T(8,128)}, u32[]{:S(2)}, u32[]{:S(2)}) collective-permute-start(f32[16,6144]{1,0:T(8,128)S(1)} %collective-permute-done.5), channel_id=1, source_target_pairs={{0,8},{8,16},{16,24},{24,0},{1,9},{9,17},{17,25},{25,1},{2,10},{10... | collective-permute-start | bytes 1179656 | tf_op jit(solution)/shard_map/ppermute | solution.py:22
  128.3 3.4 copy-start.1
  133.1 310.9 %copy-start.3 = (f32[16,64,128]{2,1,0:T(8,128)S(1)}, f32[16,64,128]{2,1,0:T(8,128)}, u32[]{:S(2)}) copy-start(f32[16,64,128]{2,1,0:T(8,128)} %copy-done.2) | copy-start | bytes 1572868
Sparse Core Ops, SparseCore 0:
  83.1 41.4 all-gather.2
  126.5 34.4 all-gather.4
